TPU v7x, 32 devices: a whole 2x2x4 slice. The times are simulated.
32 devices in a mesh: dp: 16 (over z, x, core), mp: 2 (over y).
Axes of the slice: x: 2, y: 2, z: 4, core: 2. Of those that a mesh axis runs over, the one named last changes fastest.
Arguments:
- layer_in: bfloat16 [4096, 2048], P('dp'), may hold values from -6 to 6
- out_grad: bfloat16 [4096, 2048], P('dp'), may hold values from -6 to 6
- norm_gain: bfloat16 [2, 2048], P(None, 'dp'), may hold values from 0.5 to 1.5
- norm_bias: bfloat16 [2, 2048], P(None, 'dp'), may hold values from -1.5 to 1.5
- qkv_weight: bfloat16 [3, 2048, 2048], P(None, 'dp', 'mp'), may hold values from -0.125 to 0.125
- qkv_bias: bfloat16 [3, 8, 256], P(None, 'mp', 'dp'), may hold values from -12 to 12
- out_weight: bfloat16 [2048, 2048], P('mp', 'dp'), may hold values from -1 to 1
- attn_bias: bfloat16 [2048], P('dp'), may hold values from -1.5 to 1.5
- up_weight: bfloat16 [2048, 8192], P('dp', 'mp'), may hold values from -0.125 to 0.125
- up_bias: bfloat16 [64, 128], P('mp', 'dp'), may hold values from -1.5 to 1.5
- down_weight: bfloat16 [8192, 2048], P('mp', 'dp'), may hold values from -0.0625 to 0.0625
- mlp_bias: bfloat16 [2048], P('dp'), may hold values from -1.5 to 1.5
Outputs:
- layer_out: float32 [4096, 2048], P('dp')
- in_grad: float32 [4096, 2048], P('dp')
- gain_grad: float32 [2, 2048], P(None, 'dp')
- shift_grad: float32 [2, 2048], P(None, 'dp')
- qkv_grad: float32 [3, 2048, 2048], P(None, 'dp', 'mp')
- qkv_bias_grad: float32 [3, 8, 256], P(None, 'mp', 'dp')
- out_weight_grad: float32 [2048, 2048], P('mp', 'dp')
- out_bias_grad: float32 [2048], P('dp')
- up_grad: float32 [2048, 8192], P('dp', 'mp')
- up_bias_grad: float32 [64, 128], P('mp', 'dp')
- down_grad: float32 [8192, 2048], P('mp', 'dp')
All inputs are finite; a program needn't handle non-finite values.
Results may differ from a plain program's by a relative error of at most 0.0095.
The roundings to bfloat16 on the way count: a program that leaves them out, or rounds other values in their place, can miss the bound.
Values may be sent and summed in bfloat16 or wider, within the bound.
No kernel may reach another device: no remote copies, remote signals or barrier semaphores. Data moves between devices by JAX's collectives and lax.ppermute only.
A program may use at most 256 MiB of HBM per device.

v0:
```python
import math
import jax
import jax.numpy as jnp
from jax import lax
from jax.sharding import PartitionSpec as P

HEAD = 256
ROT = 64
SEQ = 256
EPS = 1e-05
NORMAL_PEAK = 0.3989422804014327
ROOT_HALF = 0.7071067811865476


def normalize(rows_in):
    mean_row = jnp.mean(rows_in, axis=-1, keepdims=True)
    centred = rows_in - mean_row
    variance = jnp.mean(centred * centred, axis=-1, keepdims=True)
    inv_std = lax.rsqrt(variance + EPS)
    return (centred * inv_std, inv_std)


def rotary(length, half_rot, full_rot):
    position = jnp.arange(length, dtype=jnp.float32)[:, None]
    exponent = jnp.arange(half_rot, dtype=jnp.float32) * (2.0 / full_rot)
    angle = position * jnp.exp(-math.log(10000.0) * exponent)[None, :]
    return (jnp.cos(angle), jnp.sin(angle))


def turn(tensor, cosine, sine, sign):
    half_rot = cosine.shape[-1]
    lead_part = tensor[..., :half_rot]
    next_part = tensor[..., half_rot : 2 * half_rot]
    rest_part = tensor[..., 2 * half_rot :]
    cos_rows = cosine[None, :, None, :]
    sin_rows = sign * sine[None, :, None, :]
    return jnp.concatenate(
        [
            lead_part * cos_rows - next_part * sin_rows,
            next_part * cos_rows + lead_part * sin_rows,
            rest_part,
        ],
        axis=-1,
    )


def causal_scores(queries, keys_rot):
    scale = HEAD ** (-0.5)
    scores = (
        jnp.einsum("bqhe,bkhe->bhqk", queries, keys_rot, preferred_element_type=jnp.float32) * scale
    )
    length = scores.shape[-1]
    causal = lax.broadcasted_iota(jnp.int32, (length, length), 0) >= lax.broadcasted_iota(
        jnp.int32, (length, length), 1
    )
    return jnp.where(causal, scores, -jnp.inf)


def attend(queries, keys_rot, values):
    scores = causal_scores(queries, keys_rot)
    top_score = jnp.max(scores, axis=-1, keepdims=True)
    total = jnp.sum(jnp.exp(scores - top_score), axis=-1, keepdims=True)
    log_total = top_score + jnp.log(total)
    probs = jnp.exp(scores - log_total).astype(jnp.bfloat16)
    context = jnp.einsum("bhqk,bkhe->bqhe", probs, values, preferred_element_type=jnp.float32)
    return (context.astype(jnp.bfloat16), log_total)


def attend_back(queries, keys_rot, values, log_total, grad_context):
    scale = HEAD ** (-0.5)
    prob_full = jnp.exp(causal_scores(queries, keys_rot) - log_total)
    probs = prob_full.astype(jnp.bfloat16)
    grad_values = jnp.einsum(
        "bhqk,bqhe->bkhe", probs, grad_context, preferred_element_type=jnp.float32
    )
    grad_probs = jnp.einsum(
        "bqhe,bkhe->bhqk", grad_context, values, preferred_element_type=jnp.float32
    )
    grad_scores = prob_full * (grad_probs - jnp.sum(prob_full * grad_probs, axis=-1, keepdims=True))
    scores_half = grad_scores.astype(jnp.bfloat16)
    grad_queries = (
        jnp.einsum("bhqk,bkhe->bqhe", scores_half, keys_rot, preferred_element_type=jnp.float32)
        * scale
    )
    grad_keys = (
        jnp.einsum("bhqk,bqhe->bkhe", scores_half, queries, preferred_element_type=jnp.float32)
        * scale
    )
    return (grad_queries, grad_keys, grad_values)


def gelu_slope(value):
    return (
        0.5 * (1.0 + lax.erf(value * ROOT_HALF))
        + value * jnp.exp(-0.5 * value * value) * NORMAL_PEAK
    )


def contract(left, right):
    return lax.dot_general(
        left, right, (((0,), (0,)), ((), ())), preferred_element_type=jnp.float32
    )


def project_back(left, right):
    return lax.dot_general(
        left, right, (((1,), (1,)), ((), ())), preferred_element_type=jnp.float32
    )


def on_device(
    layer_in,
    out_grad,
    norm_gain,
    norm_bias,
    qkv_weight,
    qkv_bias,
    out_weight,
    attn_bias,
    up_weight,
    up_bias,
    down_weight,
    mlp_bias,
):
    (
        gain_all,
        shift_all,
        qkv_all,
        qkv_shift,
        out_all,
        attn_shift,
        up_all,
        up_shift,
        down_all,
        mlp_shift,
    ) = (
        lax.all_gather(norm_gain, "dp", axis=1, tiled=True),
        lax.all_gather(norm_bias, "dp", axis=1, tiled=True),
        lax.all_gather(qkv_weight, "dp", axis=1, tiled=True),
        lax.all_gather(qkv_bias, "dp", axis=2, tiled=True),
        lax.all_gather(out_weight, "dp", axis=1, tiled=True),
        lax.all_gather(attn_bias, "dp", axis=0, tiled=True),
        lax.all_gather(up_weight, "dp", axis=0, tiled=True),
        lax.all_gather(up_bias, "dp", axis=1, tiled=True),
        lax.all_gather(down_weight, "dp", axis=1, tiled=True),
        lax.all_gather(mlp_bias, "dp", axis=0, tiled=True),
    )
    row_count = layer_in.shape[0]
    seq_count = row_count // SEQ
    head_count = qkv_shift.shape[1]
    local_width = qkv_all.shape[2]
    inputs = layer_in.astype(jnp.float32)
    unit_rows, inv_std = normalize(inputs)
    gains = gain_all.astype(jnp.float32)
    shifts = shift_all.astype(jnp.float32)
    normed_attn = (unit_rows * gains[0] + shifts[0]).astype(jnp.bfloat16)
    normed_mlp = (unit_rows * gains[1] + shifts[1]).astype(jnp.bfloat16)
    cosine, sine = rotary(SEQ, ROT // 2, ROT)
    projected = [
        jnp.dot(normed_attn, qkv_all[index], preferred_element_type=jnp.float32)
        + qkv_shift[index].reshape(local_width).astype(jnp.float32)
        for index in range(3)
    ]
    shaped = [item.reshape(seq_count, SEQ, head_count, HEAD) for item in projected]
    queries = turn(shaped[0], cosine, sine, 1.0).astype(jnp.bfloat16)
    keys_rot = turn(shaped[1], cosine, sine, 1.0).astype(jnp.bfloat16)
    values = shaped[2].astype(jnp.bfloat16)
    context, log_total = attend(queries, keys_rot, values)
    context_rows = context.reshape(row_count, local_width)
    pre_act = jnp.dot(normed_mlp, up_all, preferred_element_type=jnp.float32) + up_shift.reshape(
        -1
    ).astype(jnp.float32)
    activated = jax.nn.gelu(pre_act, approximate=False).astype(jnp.bfloat16)
    branch_sum = jnp.dot(context_rows, out_all, preferred_element_type=jnp.float32) + jnp.dot(
        activated, down_all, preferred_element_type=jnp.float32
    )
    mixed = lax.psum(branch_sum.astype(jnp.bfloat16), "mp").astype(jnp.float32)
    layer_out = inputs + mixed + attn_shift.astype(jnp.float32) + mlp_shift.astype(jnp.float32)
    gain_back, qkv_back, out_back, up_back, down_back = (
        lax.all_gather(norm_gain, "dp", axis=1, tiled=True),
        lax.all_gather(qkv_weight, "dp", axis=1, tiled=True),
        lax.all_gather(out_weight, "dp", axis=1, tiled=True),
        lax.all_gather(up_weight, "dp", axis=0, tiled=True),
        lax.all_gather(down_weight, "dp", axis=1, tiled=True),
    )
    out_bias_grad = jnp.sum(out_grad.astype(jnp.float32), axis=0)
    down_grad = contract(activated, out_grad)
    grad_act = project_back(out_grad, down_back)
    grad_pre = grad_act * gelu_slope(pre_act)
    up_bias_grad = jnp.sum(grad_pre, axis=0).reshape(up_shift.shape)
    pre_half = grad_pre.astype(jnp.bfloat16)
    up_grad = contract(normed_mlp, pre_half)
    grad_normed_mlp = project_back(pre_half, up_back)
    out_weight_grad = contract(context_rows, out_grad)
    grad_context = (
        project_back(out_grad, out_back)
        .astype(jnp.bfloat16)
        .reshape(seq_count, SEQ, head_count, HEAD)
    )
    grad_queries, grad_keys, grad_values = attend_back(
        queries, keys_rot, values, log_total, grad_context
    )
    grad_proj = [
        turn(grad_queries, cosine, sine, -1.0).reshape(row_count, local_width),
        turn(grad_keys, cosine, sine, -1.0).reshape(row_count, local_width),
        grad_values.reshape(row_count, local_width),
    ]
    qkv_bias_grad = jnp.stack([jnp.sum(item, axis=0) for item in grad_proj]).reshape(
        3, head_count, HEAD
    )
    proj_half = [item.astype(jnp.bfloat16) for item in grad_proj]
    qkv_grad = jnp.stack([contract(normed_attn, item) for item in proj_half])
    grad_normed_attn = project_back(proj_half[0], qkv_back[0])
    grad_normed_attn = grad_normed_attn + project_back(proj_half[1], qkv_back[1])
    grad_normed_attn = grad_normed_attn + project_back(proj_half[2], qkv_back[2])
    summed_attn, summed_mlp = (
        lax.psum(grad_normed_attn.astype(jnp.bfloat16), "mp").astype(jnp.float32),
        lax.psum(grad_normed_mlp.astype(jnp.bfloat16), "mp").astype(jnp.float32),
    )
    gain_grad = jnp.stack(
        [jnp.sum(summed_attn * unit_rows, axis=0), jnp.sum(summed_mlp * unit_rows, axis=0)]
    )
    shift_grad = jnp.stack([jnp.sum(summed_attn, axis=0), jnp.sum(summed_mlp, axis=0)])
    back_gains = gain_back.astype(jnp.float32)
    grad_unit = summed_attn * back_gains[0] + summed_mlp * back_gains[1]
    in_grad = out_grad.astype(jnp.float32) + inv_std * (
        grad_unit
        - jnp.mean(grad_unit, axis=-1, keepdims=True)
        - unit_rows * jnp.mean(grad_unit * unit_rows, axis=-1, keepdims=True)
    )
    (
        gain_out,
        shift_out,
        qkv_out,
        qkv_bias_out,
        out_weight_out,
        out_bias_out,
        up_out,
        up_bias_out,
        down_out,
    ) = (
        lax.psum_scatter(gain_grad, "dp", scatter_dimension=1, tiled=True),
        lax.psum_scatter(shift_grad, "dp", scatter_dimension=1, tiled=True),
        lax.psum_scatter(qkv_grad, "dp", scatter_dimension=1, tiled=True),
        lax.psum_scatter(qkv_bias_grad, "dp", scatter_dimension=2, tiled=True),
        lax.psum_scatter(out_weight_grad, "dp", scatter_dimension=1, tiled=True),
        lax.psum_scatter(out_bias_grad, "dp", scatter_dimension=0, tiled=True),
        lax.psum_scatter(up_grad, "dp", scatter_dimension=0, tiled=True),
        lax.psum_scatter(up_bias_grad, "dp", scatter_dimension=1, tiled=True),
        lax.psum_scatter(down_grad, "dp", scatter_dimension=1, tiled=True),
    )
    return (
        layer_out,
        in_grad,
        gain_out,
        shift_out,
        qkv_out,
        qkv_bias_out,
        out_weight_out,
        out_bias_out,
        up_out,
        up_bias_out,
        down_out,
    )


def solution(mesh):
    placed = (
        P("dp", None),
        P("dp", None),
        P(None, "dp"),
        P(None, "dp"),
        P(None, "dp", "mp"),
        P(None, "mp", "dp"),
        P("mp", "dp"),
        P("dp"),
        P("dp", "mp"),
        P("mp", "dp"),
        P("mp", "dp"),
        P("dp"),
    )
    return jax.shard_map(
        on_device,
        mesh=mesh,
        in_specs=placed,
        out_specs=(
            P("dp", None),
            P("dp", None),
            P(None, "dp"),
            P(None, "dp"),
            P(None, "dp", "mp"),
            P(None, "mp", "dp"),
            P("mp", "dp"),
            P("dp"),
            P("dp", "mp"),
            P("mp", "dp"),
            P("mp", "dp"),
        ),
        check_vma=False,
    )
```

profile of v0, /device:TPU:0, one launch (start us, length us, event | category | flops | bytes accessed | tf_op | source)
XLA Modules:
  0.0 1756.7 jit_solution(10714257107157818907)
XLA Ops:
  10.9 23.5 %all_gather.41 = bf16[32,128]{0,1:T(8,128)(2,1)S(1)} all-gather(bf16[32,8]{0,1:T(8,128)(2,1)} %param.21), channel_id=1, replica_groups=mesh['dp'=16,'mp'=2] {'dp'}, dimensions={1}, use_global_device_ids=true | all-gather | bytes 8704 | tf_op jit(solution)/shard_map/all_gather | solution.py:144
  34.4 19.0 %all_gather.38 = bf16[3,4,256]{1,0,2:T(4,128)(2,1)S(1)} all-gather(bf16[3,4,16]{1,0,2:T(4,128)(2,1)S(1)} %copy.112), channel_id=1, replica_groups=mesh['dp'=16,'mp'=2] {'dp'}, dimensions={2}, use_global_device_ids=true | all-gather | bytes 6528 | tf_op jit(solution)/shard_map/all_gather | solution.py:140
  55.3 19.7 %all_gather.35 = bf16[2,2048]{1,0:T(2,128)(2,1)S(1)} all-gather(bf16[2,128]{1,0:T(2,128)(2,1)S(1)} %copy-done.29), channel_id=1, replica_groups=mesh['dp'=16,'mp'=2] {'dp'}, dimensions={1}, use_global_device_ids=true | all-gather | bytes 8704 | tf_op jit(solution)/shard_map/all_gather | solution.py:137
  75.0 18.0 %all_gather.36 = bf16[2,2048]{1,0:T(2,128)(2,1)S(1)} all-gather(bf16[2,128]{1,0:T(2,128)(2,1)S(1)} %copy-done.30), channel_id=1, replica_groups=mesh['dp'=16,'mp'=2] {'dp'}, dimensions={1}, use_global_device_ids=true | all-gather | bytes 8704 | tf_op jit(solution)/shard_map/all_gather | solution.py:138
  96.6 3.5 convolution_convert_fusion.2
  101.1 66.4 %all-gather.7.cloned.1.call-done = bf16[3,2048,1024]{2,1,0:T(8,128)(2,1)} async-done(((bf16[3,128,1024]{2,1,0:T(8,128)(2,1)}), bf16[3,2048,1024]{2,1,0:T(8,128)(2,1)}) %all-gather.7.cloned.1.call-update) | async-done | bytes 12582928 | tf_op jit(solution)/shard_map/all_gather | solution.py:139
  167.5 4.5 fusion.47
  172.0 1.7 reshape.370
  174.8 5.0 fusion.48
  179.8 2.7 reshape.369
  182.5 1.6 slice.103
  185.3 1.9 fusion.83
  188.7 3.5 fusion.50
  199.7 2.0 copy.134
  201.7 2.7 fusion.69
  204.4 2.1 copy.130
  206.5 2.3 convolution_convert_fusion.1
  208.8 1.5 fusion.82
  210.4 3.7 fusion.16
  214.1 3.5 fusion.20
  217.7 5.2 fusion.23
  222.9 71.5 %all-gather.11.cloned.1.call-done = bf16[2048,4096]{1,0:T(8,128)(2,1)} async-done(((bf16[128,4096]{1,0:T(8,128)(2,1)}), bf16[2048,4096]{1,0:T(8,128)(2,1)}) %all-gather.11.cloned.1.call-update) | async-done | bytes 16777232 | tf_op jit(solution)/shard_map/all_gather | solution.py:143
  294.4 19.0 %fusion.2 = (bf16[256,4096]{1,0:T(8,128)(2,1)}, f32[256,4096]{1,0:T(8,128)}) fusion(f32[4096]{0:T(1024)S(1)} %copy-done.27, bf16[2048,4096]{1,0:T(8,128)(2,1)} %all-gather.11.cloned.1.call-done, bf16[256,2048]{1,0:T(8,128)(2,1)S(1)} %copy-done, f32[2048]{0:T(1024)S(1)} %bitcast.169, f32[2048]{0:T(1024)S(1)} %bitcast.165, f32[256]{0:T(256)S(1)} %copy-done.24, ...), kind=kOutput, calls=%fused_computation.10 | convolution fusion | flops 4367319040 | bytes 24152064 | tf_op jit(solution)/shard_map/dot_general | solution.py:170
  313.5 111.0 %all-gather.13.cloned.1.call-done = bf16[4096,2048]{1,0:T(8,128)(2,1)} async-done(((bf16[4096,128]{1,0:T(8,128)(2,1)}), bf16[4096,2048]{1,0:T(8,128)(2,1)}) %all-gather.13.cloned.1.call-update) | async-done | bytes 16777232 | tf_op jit(solution)/shard_map/all_gather | solution.py:145
  424.5 11.0 fusion.89
  435.5 9.6 fusion.90
  445.1 11.9 convolution_convert_fusion
  457.0 5.1 fusion.22
  462.2 2.2 fusion.66
  464.4 1.8 fusion.68
  467.5 78.9 %all-reduce.6.cloned.1.call-done = (bf16[256,2048]{1,0:T(8,128)(2,1)}, bf16[256,2048]{1,0:T(8,128)(2,1)}, bf16[256,2048]{1,0:T(8,128)(2,1)}) async-done(((bf16[256,2048]{1,0:T(8,128)(2,1)}, bf16[256,2048]{1,0:T(8,128)(2,1)}, bf16[256,2048]{1,0:T(8,128)(2,1)}), (bf16[256,2048]{1,0:T(8,128)(2,1)}, bf16[256,2048]{1,0:T(8,128)(2,1)}, bf16[256,2048]{1,0:T(8,128)(2,1)})) %all-reduce.6.cloned.1.call-update) | async-done | bytes 3145744 | tf_op jit(solution)/shard_map/psum | solution.py:177
  546.4 3.1 fusion.46
  552.4 4.6 fusion.91
  560.9 1.4 convolution_bitcast_fusion.2
  562.4 8.7 pad_maximum_fusion
  571.2 14.9 fusion.51
  586.2 14.8 fusion.92
  603.5 21.4 %all-gather = bf16[16,1,128]{2,1,0:T(2,128)(2,1)S(1)} all-gather(bf16[1,1,128]{2,1,0:T(2,128)(2,1)S(1)} %bitcast.187), channel_id=1, replica_groups=mesh['dp'=16,'mp'=2] {'dp'}, dimensions={0}, use_global_device_ids=true | all-gather | bytes 4352 | tf_op jit(solution)/shard_map/all_gather | solution.py:142
  624.9 17.4 all-gather.1
  643.9 5.3 convert_reduce_fusion.3
  649.2 59.1 %all-reduce.2 = (f32[2048]{0:T(1024)S(1)}, f32[32,128]{1,0:T(8,128)S(1)}) all-reduce(f32[2048]{0:T(1024)S(1)} %get-tuple-element.74, f32[32,128]{1,0:T(8,128)S(1)} %bitcast.183), channel_id=7, replica_groups=mesh['dp'=16,'mp'=2] {'dp'}, use_global_device_ids=true, to_apply=%region_23.24.clone | all-reduce | flops 6144 | bytes 49152
  709.6 1.5 copy.149
  711.1 14.9 reduce-scatter.23.cloned.1.call-done
  726.0 1.5 copy.147
  727.5 105.8 %reduce-scatter.17.cloned.1.call-done = f32[1024,128]{1,0:T(8,128)} async-done(((f32[1024,2048]{1,0:T(8,128)}), f32[1024,128]{1,0:T(8,128)}) %reduce-scatter.17.cloned.1.call-update) | async-done | bytes 524304 | tf_op jit(solution)/shard_map/reduce_scatter | solution.py:246
  833.3 247.5 %reduce-scatter.15.cloned.1.call-done = f32[3,128,1024]{2,1,0:T(8,128)} async-done(((f32[3,2048,1024]{2,1,0:T(8,128)}), f32[3,128,1024]{2,1,0:T(8,128)}) %reduce-scatter.15.cloned.1.call-update) | async-done | bytes 1572880 | tf_op jit(solution)/shard_map/reduce_scatter | solution.py:244
  1080.8 334.5 %reduce-scatter.19.cloned.1.call-done = f32[128,4096]{1,0:T(8,128)} async-done(((f32[2048,4096]{1,0:T(8,128)}), f32[128,4096]{1,0:T(8,128)}) %reduce-scatter.19.cloned.1.call-update) | async-done | bytes 2097168 | tf_op jit(solution)/shard_map/reduce_scatter | solution.py:248
  1415.3 334.1 %reduce-scatter.21.cloned.1.call-done = f32[4096,128]{1,0:T(8,128)} async-done(((f32[4096,2048]{1,0:T(8,128)}), f32[4096,128]{1,0:T(8,128)}) %reduce-scatter.21.cloned.1.call-update) | async-done | bytes 2097168 | tf_op jit(solution)/shard_map/reduce_scatter | solution.py:250
  (151 shorter events, 33.6 us)
Async XLA Ops:
  7.2 48.1 %copy-start.29 = (bf16[2,128]{1,0:T(2,128)(2,1)S(1)}, bf16[2,128]{1,0:T(2,128)(2,1)}, u32[]{:S(2)}) copy-start(bf16[2,128]{1,0:T(2,128)(2,1)} %param.14) | copy-start | bytes 1540
  7.2 67.8 %copy-start.30 = (bf16[2,128]{1,0:T(2,128)(2,1)S(1)}, bf16[2,128]{1,0:T(2,128)(2,1)}, u32[]{:S(2)}) copy-start(bf16[2,128]{1,0:T(2,128)(2,1)} %param.15) | copy-start | bytes 1540
  7.2 86.4 %copy-start = (bf16[256,2048]{1,0:T(8,128)(2,1)S(1)}, bf16[256,2048]{1,0:T(8,128)(2,1)}, u32[]{:S(2)}) copy-start(bf16[256,2048]{1,0:T(8,128)(2,1)} %param.12) | copy-start | bytes 3145732
  7.2 89.4 %copy-start.1 = (bf16[256,2048]{1,0:T(8,128)(2,1)S(1)}, bf16[256,2048]{1,0:T(8,128)(2,1)}, u32[]{:S(2)}) copy-start(bf16[256,2048]{1,0:T(8,128)(2,1)} %param.13) | copy-start | bytes 3145732
  7.2 89.4 %all-gather.9.cloned.1.call-start = ((), (), s32[]{:S(2)}) async-start(), calls=%async_computation.8 | async-start | bytes 4456448 | tf_op jit(solution)/shard_map/all_gather | solution.py:141
  8.0 159.6 %all-gather.7.cloned.1.call-start = ((), (), s32[]{:S(2)}) async-start(), calls=%async_computation.7 | async-start | bytes 13369344 | tf_op jit(solution)/shard_map/all_gather | solution.py:139
  8.7 285.7 %all-gather.11.cloned.1.call-start = ((), (), s32[]{:S(2)}) async-start(), calls=%async_computation.9 | async-start | bytes 17825792 | tf_op jit(solution)/shard_map/all_gather | solution.py:143
  9.4 415.1 %all-gather.13.cloned.1.call-start = ((), (), s32[]{:S(2)}) async-start(), calls=%async_computation.10 | async-start | bytes 17825792 | tf_op jit(solution)/shard_map/all_gather | solution.py:145
  10.0 536.3 %all-reduce.6.cloned.1.call-start = ((), (), s32[]{:S(2)}) async-start(), calls=%async_computation.18 | async-start | bytes 6291456 | tf_op jit(solution)/shard_map/psum | solution.py:177
  93.9 73.7 %copy-start.19 = (f32[256]{0:T(256)}, f32[256]{0:T(256)S(1)}, u32[]{:S(2)}) copy-start(f32[256]{0:T(256)S(1)} %broadcast_multiply_fusion.3) | copy-start | bytes 3076
  94.3 73.2 %copy-start.22 = (f32[256]{0:T(256)}, f32[256]{0:T(256)S(1)}, u32[]{:S(2)}) copy-start(f32[256]{0:T(256)S(1)} %add_rsqrt_fusion) | copy-start | bytes 3076
  185.3 2.2 copy-start.26
  187.2 1.5 copy-start.20
  187.2 1.5 copy-start.23
  187.2 1.5 copy-start.28
  188.7 3.6 copy-start.8
  192.3 1.3 copy-start.17
  196.1 1.3 copy-start.3
  197.4 0.8 copy-start.6
  197.4 1.0 copy-start.7
  206.5 3.8 copy-start.13
  210.3 7.3 copy-start.15
  210.3 3.7 copy-start.4
  217.6 76.8 %copy-start.18 = (f32[1,2048]{1,0:T(1,128)S(1)}, f32[1,2048]{1,0:T(1,128)}, u32[]{:S(2)}) copy-start(f32[1,2048]{1,0:T(1,128)} %get-tuple-element.91) | copy-start | bytes 24580
  217.6 76.8 %copy-start.21 = (f32[256]{0:T(256)S(1)}, f32[256]{0:T(256)}, u32[]{:S(2)}) copy-start(f32[256]{0:T(256)} %copy-done.19) | copy-start | bytes 3076
  217.6 76.8 %copy-start.24 = (f32[256]{0:T(256)S(1)}, f32[256]{0:T(256)}, u32[]{:S(2)}) copy-start(f32[256]{0:T(256)} %copy-done.22) | copy-start | bytes 3076
  217.6 76.8 %copy-start.25 = (f32[1,2048]{1,0:T(1,128)S(1)}, f32[1,2048]{1,0:T(1,128)}, u32[]{:S(2)}) copy-start(f32[1,2048]{1,0:T(1,128)} %get-tuple-element.93) | copy-start | bytes 24580
  217.7 76.8 %copy-start.27 = (f32[4096]{0:T(1024)S(1)}, f32[4096]{0:T(1024)}, u32[]{:S(2)}) copy-start(f32[4096]{0:T(1024)} %bitcast_convert_fusion) | copy-start | bytes 49156
  424.5 11.0 copy-start.10
  445.1 12.0 copy-start.11
  462.1 2.3 copy-start.2
  462.1 180.2 %reduce-scatter.27.cloned.1.call-start = ((), (), s32[]{:S(2)}) async-start(), calls=%async_computation.17 | async-start | bytes 139264
  466.5 85.9 %copy-start.12 = (bf16[4,256,256]{2,1,0:T(8,128)(2,1)S(1)}, bf16[4,256,256]{2,1,0:T(8,128)(2,1)}, u32[]{:S(2)}) copy-start(bf16[4,256,256]{2,1,0:T(8,128)(2,1)} %convolution_convert_fusion.1) | copy-start | bytes 1572868
  467.4 242.2 %reduce-scatter.25.cloned.1.call-start = ((), (), s32[]{:S(2)}) async-start(), calls=%async_computation.16 | async-start | bytes 1114112
  550.9 175.1 %reduce-scatter.23.cloned.1.call-start = ((), (), s32[]{:S(2)}) async-start(), calls=%async_computation.15 | async-start | bytes 1114112
  552.4 281.0 %reduce-scatter.17.cloned.1.call-start = ((), (), s32[]{:S(2)}) async-start(), calls=%async_computation.12 | async-start | bytes 8912896 | tf_op jit(solution)/shard_map/reduce_scatter | solution.py:246
  557.0 1.0 copy-start.16
  557.0 2.5 copy-start.5
  557.0 523.8 %reduce-scatter.15.cloned.1.call-start = ((), (), s32[]{:S(2)}) async-start(), calls=%async_computation.11 | async-start | bytes 26738688 | tf_op jit(solution)/shard_map/reduce_scatter | solution.py:244
  559.5 1.4 copy-start.14
  571.1 844.2 %reduce-scatter.19.cloned.1.call-start = ((), (), s32[]{:S(2)}) async-start(), calls=%async_computation.13 | async-start | bytes 35651584 | tf_op jit(solution)/shard_map/reduce_scatter | solution.py:248
  586.1 1163.3 %reduce-scatter.21.cloned.1.call-start = ((), (), s32[]{:S(2)}) async-start(), calls=%async_computation.14 | async-start | bytes 35651584 | tf_op jit(solution)/shard_map/reduce_scatter | solution.py:250
  601.0 0.7 copy-start.33
  601.0 2.5 copy-start.31
  601.0 23.9 %copy-start.32 = (bf16[128]{0:T(256)(128)(2,1)S(1)}, bf16[128]{0:T(256)(128)(2,1)}, u32[]{:S(2)}) copy-start(bf16[128]{0:T(256)(128)(2,1)} %param.23) | copy-start | bytes 772
  601.0 42.9 %copy-start.9 = (bf16[256,2048]{1,0:T(8,128)(2,1)S(1)}, bf16[256,2048]{1,0:T(8,128)(2,1)}, u32[]{:S(2)}) copy-start(bf16[256,2048]{1,0:T(8,128)(2,1)} %get-tuple-element.64) | copy-start | bytes 3145732
Sparse Core Ops, SparseCore 0:
  10.2 56.1 all-gather.8
  68.6 98.8 all-gather.6
  169.7 124.6 all-gather.10
  296.4 128.0 all-gather.12
  462.3 84.0 all-reduce.5
  549.7 55.5 reduce-scatter.26
  608.9 56.6 reduce-scatter.24
  669.2 56.7 reduce-scatter.22
  730.7 102.6 reduce-scatter.16
  837.9 242.9 reduce-scatter.14
  1085.7 329.5 reduce-scatter.18
  1420.0 329.4 reduce-scatter.20
where the time goes:
time: 1770 us; the launch traced here: 1760 us
  waiting for transfers between devices  1370 us (77%)
  blocking collectives  178 us (10%)
  matrix products  131 us (7%)
  local copies, waits for them, and re-layouts  33.6 us (2%)
  other arithmetic  29.5 us (2%)
    reduce_scatter x1, waiting for transfers between devices, on_device(): lax.psum_scatter(up_grad, 'dp', scatter_dimension=0, tiled=True)  334 us
    reduce_scatter x1, waiting for transfers between devices, on_device(): lax.psum_scatter(down_grad, 'dp', scatter_dimension=1, tiled=True)  334 us
    reduce_scatter x1, waiting for transfers between devices, on_device(): lax.psum_scatter(qkv_grad, 'dp', scatter_dimension=1, tiled=True)  247 us
    all_gather x1, waiting for transfers between devices, on_device(): lax.all_gather(down_weight, 'dp', axis=1, tiled=True)  111 us
    reduce_scatter x1, waiting for transfers between devices, on_device(): lax.psum_scatter(out_weight_grad, 'dp', scatter_dimension=1, tiled=True)  106 us
    psum x1, waiting for transfers between devices, on_device(): mixed = lax.psum(branch_sum.astype(jnp.bfloat16), 'mp').astype(jnp.float32)  78.9 us
    all_gather x1, waiting for transfers between devices, on_device(): lax.all_gather(up_weight, 'dp', axis=0, tiled=True)  71.5 us
    all_gather x1, waiting for transfers between devices, on_device(): lax.all_gather(qkv_weight, 'dp', axis=1, tiled=True)  66.4 us
  transfers between devices with their start and end apart: 12, of which 9 were waited for; matrix products, arithmetic and copies ran while one was open for 9% of the time, Pallas kernels for 0%

commit v1 on v0

--- a/solution.py
+++ b/solution.py
@@ -10,6 +10,27 @@
 EPS = 1e-05
 NORMAL_PEAK = 0.3989422804014327
 ROOT_HALF = 0.7071067811865476
+
+
+def collect(x, axis, dim):
+    size, here, rows = (lax.axis_size(axis), lax.axis_index(axis), x.shape[dim])
+    upward = [(i, (i + 1) % size) for i in range(size)]
+    downward = [(i, (i - 1) % size) for i in range(size)]
+    result = jnp.zeros((*x.shape[:dim], size * rows, *x.shape[dim + 1 :]), x.dtype)
+    result = lax.dynamic_update_slice_in_dim(result, x, here * rows, axis=dim)
+    from_left = from_right = x
+    halfway = size // 2
+    for step in range(1, halfway + 1):
+        from_left = lax.ppermute(from_left, axis, upward)
+        result = lax.dynamic_update_slice_in_dim(
+            result, from_left, (here - step) % size * rows, axis=dim
+        )
+        if step < size - halfway:
+            from_right = lax.ppermute(from_right, axis, downward)
+            result = lax.dynamic_update_slice_in_dim(
+                result, from_right, (here + step) % size * rows, axis=dim
+            )
+    return result
 
 
 def normalize(rows_in):
@@ -142,7 +163,7 @@
         lax.all_gather(attn_bias, "dp", axis=0, tiled=True),
         lax.all_gather(up_weight, "dp", axis=0, tiled=True),
         lax.all_gather(up_bias, "dp", axis=1, tiled=True),
-        lax.all_gather(down_weight, "dp", axis=1, tiled=True),
+        collect(down_weight, "dp", 1),
         lax.all_gather(mlp_bias, "dp", axis=0, tiled=True),
     )
     row_count = layer_in.shape[0]

time: 1770 us -> 1840 us (1.040)
  blocking collectives: 178 us -> 240 us
  waiting for transfers between devices: 1370 us -> 1320 us
  local copies, waits for them, and re-layouts: 33.6 us -> 65.6 us
  starting transfers between devices: 0.7 us -> 26.2 us
    ppermute x0 -> x15, waiting for transfers between devices: none -> 113 us  [the longest x7 99 us: collect(): from_right = lax.ppermute(from_right, axis, downward)]
    all_gather x1, waiting for transfers between devices: 71.5 us -> 0.01 us  [on_device(): lax.all_gather(up_weight, 'dp', axis=0, tiled=True)]
    all_gather x1, waiting for transfers between devices: 66.4 us -> 0.01 us  [on_device(): lax.all_gather(qkv_weight, 'dp', axis=1, tiled=True)]
    all_gather x1, blocking collectives: 18 us -> 52.2 us  [on_device(): lax.all_gather(norm_bias, 'dp', axis=1, tiled=True)]
    ppermute x0 -> x15, starting transfers between devices: none -> 25.5 us  [the longest x7 23.8 us: collect(): from_right = lax.ppermute(from_right, axis, downward)]
    dynamic_update_slice x0 -> x16, local copies, waits for them, and re-layouts: none -> 23.1 us  [the longest x8 12.7 us: collect(): lax.dynamic_update_slice_in_dim(result, from_left, (here - step) % size *...]
    all_gather x1, waiting for transfers between devices: 111 us -> 89.1 us  [on_device(): lax.all_gather(down_weight, 'dp', axis=1, tiled=True)]
  transfers between devices with their start and end apart: 12 -> 27, of which waited for: 9 -> 15; matrix products, arithmetic and copies ran while one was open for 9% -> 11% of each run, Pallas kernels for 0% -> 0%
where the time goes in v1:
time: 1840 us; the launch traced here: 1830 us
  waiting for transfers between devices  1320 us (72%)
  blocking collectives  240 us (13%)
  matrix products  127 us (7%)
  local copies, waits for them, and re-layouts  65.6 us (4%)
  other arithmetic  32.3 us (2%)
  starting transfers between devices  26.2 us (1%)
    reduce_scatter x1, waiting for transfers between devices, on_device(): lax.psum_scatter(up_grad, 'dp', scatter_dimension=0, tiled=True)  334 us
    reduce_scatter x1, waiting for transfers between devices, on_device(): lax.psum_scatter(down_grad, 'dp', scatter_dimension=1, tiled=True)  334 us
    reduce_scatter x1, waiting for transfers between devices, on_device(): lax.psum_scatter(qkv_grad, 'dp', scatter_dimension=1, tiled=True)  248 us
    reduce_scatter x1, waiting for transfers between devices, on_device(): lax.psum_scatter(out_weight_grad, 'dp', scatter_dimension=1, tiled=True)  106 us
    ppermute x7, waiting for transfers between devices, collect(): from_right = lax.ppermute(from_right, axis, downward)  99 us
    all_gather x1, waiting for transfers between devices, on_device(): lax.all_gather(down_weight, 'dp', axis=1, tiled=True)  89.1 us
    psum x1, waiting for transfers between devices, on_device(): mixed = lax.psum(branch_sum.astype(jnp.bfloat16), 'mp').astype(jnp.float32)  78.9 us
    unnamed x1, blocking collectives  59.1 us
  transfers between devices with their start and end apart: 27, of which 15 were waited for; matrix products, arithmetic and copies ran while one was open for 11% of the time, Pallas kernels for 0%

profile of v1, /device:TPU:0, one launch (start us, length us, event | category | flops | bytes accessed | tf_op | source)
XLA Modules:
  0.0 1829.3 jit_solution(1286113071052956247)
XLA Ops:
  10.6 5.0 collective-permute-start.1
  16.4 37.0 %all_gather.37 = bf16[3,4,256]{1,0,2:T(4,128)(2,1)S(1)} all-gather(bf16[3,4,16]{1,0,2:T(4,128)(2,1)S(1)} %copy.112), channel_id=1, replica_groups=mesh['dp'=16,'mp'=2] {'dp'}, dimensions={2}, use_global_device_ids=true | all-gather | bytes 6528 | tf_op jit(solution)/shard_map/all_gather | solution.py:161
  55.5 20.0 %all_gather.40 = bf16[32,128]{0,1:T(8,128)(2,1)S(1)} all-gather(bf16[32,8]{0,1:T(8,128)(2,1)S(1)} %copy-done.30), channel_id=1, replica_groups=mesh['dp'=16,'mp'=2] {'dp'}, dimensions={1}, use_global_device_ids=true | all-gather | bytes 8704 | tf_op jit(solution)/shard_map/all_gather | solution.py:165
  77.6 33.3 %all_gather.34 = bf16[2,2048]{1,0:T(2,128)(2,1)S(1)} all-gather(bf16[2,128]{1,0:T(2,128)(2,1)S(1)} %copy-done.31), channel_id=1, replica_groups=mesh['dp'=16,'mp'=2] {'dp'}, dimensions={1}, use_global_device_ids=true | all-gather | bytes 8704 | tf_op jit(solution)/shard_map/all_gather | solution.py:158
  117.1 52.2 %all_gather.35 = bf16[2,2048]{1,0:T(2,128)(2,1)S(1)} all-gather(bf16[2,128]{1,0:T(2,128)(2,1)} %param.15), channel_id=1, replica_groups=mesh['dp'=16,'mp'=2] {'dp'}, dimensions={1}, use_global_device_ids=true | all-gather | bytes 8704 | tf_op jit(solution)/shard_map/all_gather | solution.py:159
  170.6 6.0 broadcast_in_dim.12
  179.3 20.1 %collective-permute-done.5 = bf16[4096,128]{1,0:T(8,128)(2,1)S(1)} collective-permute-done((bf16[4096,128]{1,0:T(8,128)(2,1)}, bf16[4096,128]{1,0:T(8,128)(2,1)S(1)}, u32[]{:S(2)}, u32[]{:S(2)}) %collective-permute-start.5) | collective-permute-done | bytes 1048608 | tf_op jit(solution)/shard_map/ppermute | solution.py:29
  199.5 4.5 collective-permute-start.7
  207.4 2.5 constant_dynamic-update-slice_fusion.11
  209.9 17.4 collective-permute-done.7
  227.3 4.6 collective-permute-start.9
  235.4 6.4 collective-permute-done.8
  242.9 17.7 collective-permute-done.9
  260.6 4.6 collective-permute-start.11
  270.7 26.0 %collective-permute-done.11 = bf16[4096,128]{1,0:T(8,128)(2,1)S(1)} collective-permute-done((bf16[4096,128]{1,0:T(8,128)(2,1)S(1)}, bf16[4096,128]{1,0:T(8,128)(2,1)S(1)}, u32[]{:S(2)}, u32[]{:S(2)}) %collective-permute-start.11) | collective-permute-done | bytes 1048608 | tf_op jit(solution)/shard_map/ppermute | solution.py:29
  296.7 4.6 collective-permute-start.13
  303.6 5.5 collective-permute-done.12
  310.5 17.7 collective-permute-done.13
  329.3 4.3 convolution_convert_fusion.2
  337.9 4.5 fusion.48
  344.1 4.5 fusion.47
  348.6 2.7 reshape.370
  356.0 3.8 fusion.50
  369.4 2.7 fusion.69
  378.2 2.6 fusion.90
  380.8 3.6 fusion.16
  384.4 3.5 fusion.20
  388.0 5.0 fusion.23
  393.1 18.4 %fusion.2 = (bf16[256,4096]{1,0:T(8,128)(2,1)S(1)}, f32[256,4096]{1,0:T(8,128)}) fusion(f32[4096]{0:T(1024)S(1)} %copy-done.28, bf16[2048,4096]{1,0:T(8,128)(2,1)} %all-gather.11.cloned.1.call-done, bf16[256,2048]{1,0:T(8,128)(2,1)S(1)} %copy-done, f32[2048]{0:T(1024)S(1)} %bitcast.169, f32[2048]{0:T(1024)S(1)} %bitcast.165, f32[256]{0:T(256)S(1)} %copy-done.25, ...), kind=kOutput, calls=%fused_computation.10 | convolution fusion | flops 4367319040 | bytes 24152064 | tf_op jit(solution)/shard_map/dot_general | solution.py:191
  412.8 9.4 fusion.22
  422.2 89.1 %all-gather.13.cloned.1.call-done = bf16[4096,2048]{1,0:T(8,128)(2,1)} async-done(((bf16[4096,128]{1,0:T(8,128)(2,1)}), bf16[4096,2048]{1,0:T(8,128)(2,1)}) %all-gather.13.cloned.1.call-update) | async-done | bytes 16777232 | tf_op jit(solution)/shard_map/all_gather | solution.py:205
  511.4 11.0 fusion.89
  522.4 12.0 convolution_convert_fusion
  539.6 78.9 %all-reduce.6.cloned.1.call-done = (bf16[256,2048]{1,0:T(8,128)(2,1)}, bf16[256,2048]{1,0:T(8,128)(2,1)}, bf16[256,2048]{1,0:T(8,128)(2,1)}) async-done(((bf16[256,2048]{1,0:T(8,128)(2,1)}, bf16[256,2048]{1,0:T(8,128)(2,1)}, bf16[256,2048]{1,0:T(8,128)(2,1)}), (bf16[256,2048]{1,0:T(8,128)(2,1)}, bf16[256,2048]{1,0:T(8,128)(2,1)}, bf16[256,2048]{1,0:T(8,128)(2,1)})) %all-reduce.6.cloned.1.call-update) | async-done | bytes 3145744 | tf_op jit(solution)/shard_map/psum | solution.py:198
  618.5 3.1 fusion.46
  624.6 4.6 fusion.91
  634.5 8.7 pad_maximum_fusion
  643.3 14.9 fusion.51
  658.3 14.8 fusion.92
  673.8 21.4 %all-gather = bf16[16,1,128]{2,1,0:T(2,128)(2,1)S(1)} all-gather(bf16[1,1,128]{2,1,0:T(2,128)(2,1)S(1)} %bitcast.187), channel_id=1, replica_groups=mesh['dp'=16,'mp'=2] {'dp'}, dimensions={0}, use_global_device_ids=true | all-gather | bytes 4352 | tf_op jit(solution)/shard_map/all_gather | solution.py:163
  695.1 17.5 all-gather.1
  716.0 5.3 convert_reduce_fusion.3
  721.3 59.1 %all-reduce.2 = (f32[2048]{0:T(1024)S(1)}, f32[32,128]{1,0:T(8,128)S(1)}) all-reduce(f32[2048]{0:T(1024)S(1)} %get-tuple-element.74, f32[32,128]{1,0:T(8,128)S(1)} %bitcast.183), channel_id=7, replica_groups=mesh['dp'=16,'mp'=2] {'dp'}, use_global_device_ids=true, to_apply=%region_23.24.clone | all-reduce | flops 6144 | bytes 49152
  783.2 15.6 reduce-scatter.23.cloned.1.call-done
  800.3 105.8 %reduce-scatter.17.cloned.1.call-done = f32[1024,128]{1,0:T(8,128)} async-done(((f32[1024,2048]{1,0:T(8,128)}), f32[1024,128]{1,0:T(8,128)}) %reduce-scatter.17.cloned.1.call-update) | async-done | bytes 524304 | tf_op jit(solution)/shard_map/reduce_scatter | solution.py:267
  906.0 247.5 %reduce-scatter.15.cloned.1.call-done = f32[3,128,1024]{2,1,0:T(8,128)} async-done(((f32[3,2048,1024]{2,1,0:T(8,128)}), f32[3,128,1024]{2,1,0:T(8,128)}) %reduce-scatter.15.cloned.1.call-update) | async-done | bytes 1572880 | tf_op jit(solution)/shard_map/reduce_scatter | solution.py:265
  1153.6 334.5 %reduce-scatter.19.cloned.1.call-done = f32[128,4096]{1,0:T(8,128)} async-done(((f32[2048,4096]{1,0:T(8,128)}), f32[128,4096]{1,0:T(8,128)}) %reduce-scatter.19.cloned.1.call-update) | async-done | bytes 2097168 | tf_op jit(solution)/shard_map/reduce_scatter | solution.py:269
  1488.1 334.1 %reduce-scatter.21.cloned.1.call-done = f32[4096,128]{1,0:T(8,128)} async-done(((f32[4096,2048]{1,0:T(8,128)}), f32[4096,128]{1,0:T(8,128)}) %reduce-scatter.21.cloned.1.call-update) | async-done | bytes 2097168 | tf_op jit(solution)/shard_map/reduce_scatter | solution.py:271
  (204 shorter events, 84.7 us)
Async XLA Ops:
  7.2 47.4 %copy-start = (bf16[256,2048]{1,0:T(8,128)(2,1)S(1)}, bf16[256,2048]{1,0:T(8,128)(2,1)}, u32[]{:S(2)}) copy-start(bf16[256,2048]{1,0:T(8,128)(2,1)} %param.12) | copy-start | bytes 3145732
  7.2 48.3 %copy-start.30 = (bf16[32,8]{0,1:T(8,128)(2,1)S(1)}, bf16[32,8]{0,1:T(8,128)(2,1)}, u32[]{:S(2)}) copy-start(bf16[32,8]{0,1:T(8,128)(2,1)} %param.21) | copy-start | bytes 1540
  7.2 70.4 %copy-start.31 = (bf16[2,128]{1,0:T(2,128)(2,1)S(1)}, bf16[2,128]{1,0:T(2,128)(2,1)}, u32[]{:S(2)}) copy-start(bf16[2,128]{1,0:T(2,128)(2,1)} %param.14) | copy-start | bytes 1540
  7.2 322.1 %all-gather.9.cloned.1.call-start = ((), (), s32[]{:S(2)}) async-start(), calls=%async_computation.8 | async-start | bytes 4456448 | tf_op jit(solution)/shard_map/all_gather | solution.py:162
  7.9 330.0 %all-gather.7.cloned.1.call-start = ((), (), s32[]{:S(2)}) async-start(), calls=%async_computation.7 | async-start | bytes 13369344 | tf_op jit(solution)/shard_map/all_gather | solution.py:160
  8.7 384.3 %all-gather.11.cloned.1.call-start = ((), (), s32[]{:S(2)}) async-start(), calls=%async_computation.9 | async-start | bytes 17825792 | tf_op jit(solution)/shard_map/all_gather | solution.py:164
  9.4 501.9 %all-gather.13.cloned.1.call-start = ((), (), s32[]{:S(2)}) async-start(), calls=%async_computation.10 | async-start | bytes 17825792 | tf_op jit(solution)/shard_map/all_gather | solution.py:205
  10.0 608.5 %all-reduce.6.cloned.1.call-start = ((), (), s32[]{:S(2)}) async-start(), calls=%async_computation.18 | async-start | bytes 6291456 | tf_op jit(solution)/shard_map/psum | solution.py:198
  10.0 66.7 %collective-permute-start = (bf16[4096,128]{1,0:T(8,128)(2,1)}, bf16[4096,128]{1,0:T(8,128)(2,1)S(1)}, u32[]{:S(2)}, u32[]{:S(2)}) collective-permute-start(bf16[4096,128]{1,0:T(8,128)(2,1)} %param.22), channel_id=1, source_target_pairs={{0,2},{2,4},{4,6},{6,8},{8,10},{10,12},{12,14},{14,16},{16,18},{18... | collective-permute-start | bytes 3145736 | tf_op jit(solution)/shard_map/ppermute | solution.py:24
  10.6 100.9 %collective-permute-start.1 = (bf16[4096,128]{1,0:T(8,128)(2,1)}, bf16[4096,128]{1,0:T(8,128)(2,1)S(1)}, u32[]{:S(2)}, u32[]{:S(2)}) collective-permute-start(bf16[4096,128]{1,0:T(8,128)(2,1)} %param.22), channel_id=1, source_target_pairs={{0,30},{2,0},{4,2},{6,4},{8,6},{10,8},{12,10},{14,12},{16,14},{18,... | collective-permute-start | bytes 3145736 | tf_op jit(solution)/shard_map/ppermute | solution.py:29
  55.4 55.6 %copy-start.21 = (f32[256]{0:T(256)}, f32[256]{0:T(256)S(1)}, u32[]{:S(2)}) copy-start(f32[256]{0:T(256)S(1)} %broadcast_multiply_fusion.3) | copy-start | bytes 3076
  76.8 36.3 %collective-permute-start.2 = (bf16[4096,128]{1,0:T(8,128)(2,1)S(1)}, bf16[4096,128]{1,0:T(8,128)(2,1)}, u32[]{:S(2)}, u32[]{:S(2)}) collective-permute-start(bf16[4096,128]{1,0:T(8,128)(2,1)S(1)} %collective-permute-done), channel_id=1, source_target_pairs={{0,2},{2,4},{4,6},{6,8},{8,10},{10,12},{12,14},{14,16},{16,18},{18... | collective-permute-start | bytes 3145736 | tf_op jit(solution)/shard_map/ppermute | solution.py:24
  111.5 58.4 %collective-permute-start.3 = (bf16[4096,128]{1,0:T(8,128)(2,1)S(1)}, bf16[4096,128]{1,0:T(8,128)(2,1)}, u32[]{:S(2)}, u32[]{:S(2)}) collective-permute-start(bf16[4096,128]{1,0:T(8,128)(2,1)S(1)} %collective-permute-done.1), channel_id=1, source_target_pairs={{0,30},{2,0},{4,2},{6,4},{8,6},{10,8},{12,10},{14,12},{16,14},{18,... | collective-permute-start | bytes 3145736 | tf_op jit(solution)/shard_map/ppermute | solution.py:29
  113.1 64.7 %collective-permute-start.4 = (bf16[4096,128]{1,0:T(8,128)(2,1)}, bf16[4096,128]{1,0:T(8,128)(2,1)}, u32[]{:S(2)}, u32[]{:S(2)}) collective-permute-start(bf16[4096,128]{1,0:T(8,128)(2,1)} %collective-permute-done.2), channel_id=1, source_target_pairs={{0,2},{2,4},{4,6},{6,8},{8,10},{10,12},{12,14},{14,16},{16,18},{18... | collective-permute-start | bytes 3145736 | tf_op jit(solution)/shard_map/ppermute | solution.py:24
  169.9 29.5 %collective-permute-start.5 = (bf16[4096,128]{1,0:T(8,128)(2,1)}, bf16[4096,128]{1,0:T(8,128)(2,1)S(1)}, u32[]{:S(2)}, u32[]{:S(2)}) collective-permute-start(bf16[4096,128]{1,0:T(8,128)(2,1)} %collective-permute-done.3), channel_id=1, source_target_pairs={{0,30},{2,0},{4,2},{6,4},{8,6},{10,8},{12,10},{14,12},{16,14},{18,... | collective-permute-start | bytes 3145736 | tf_op jit(solution)/shard_map/ppermute | solution.py:29
  170.6 6.0 copy-start.11
  177.8 29.7 %collective-permute-start.6 = (bf16[4096,128]{1,0:T(8,128)(2,1)}, bf16[4096,128]{1,0:T(8,128)(2,1)S(1)}, u32[]{:S(2)}, u32[]{:S(2)}) collective-permute-start(bf16[4096,128]{1,0:T(8,128)(2,1)} %collective-permute-done.4), channel_id=1, source_target_pairs={{0,2},{2,4},{4,6},{6,8},{8,10},{10,12},{12,14},{14,16},{16,18},{18... | collective-permute-start | bytes 3145736 | tf_op jit(solution)/shard_map/ppermute | solution.py:24
  199.5 27.9 %collective-permute-start.7 = (bf16[4096,128]{1,0:T(8,128)(2,1)S(1)}, bf16[4096,128]{1,0:T(8,128)(2,1)S(1)}, u32[]{:S(2)}, u32[]{:S(2)}) collective-permute-start(bf16[4096,128]{1,0:T(8,128)(2,1)S(1)} %collective-permute-done.5), channel_id=1, source_target_pairs={{0,30},{2,0},{4,2},{6,4},{8,6},{10,8},{12,10},{14,12},{16,14},{18,... | collective-permute-start | bytes 3145736 | tf_op jit(solution)/shard_map/ppermute | solution.py:29
  207.4 34.3 %collective-permute-start.8 = (bf16[4096,128]{1,0:T(8,128)(2,1)S(1)}, bf16[4096,128]{1,0:T(8,128)(2,1)S(1)}, u32[]{:S(2)}, u32[]{:S(2)}) collective-permute-start(bf16[4096,128]{1,0:T(8,128)(2,1)S(1)} %collective-permute-done.6), channel_id=1, source_target_pairs={{0,2},{2,4},{4,6},{6,8},{8,10},{10,12},{12,14},{14,16},{16,18},{18... | collective-permute-start | bytes 3145736 | tf_op jit(solution)/shard_map/ppermute | solution.py:24
  227.3 33.3 %collective-permute-start.9 = (bf16[4096,128]{1,0:T(8,128)(2,1)S(1)}, bf16[4096,128]{1,0:T(8,128)(2,1)S(1)}, u32[]{:S(2)}, u32[]{:S(2)}) collective-permute-start(bf16[4096,128]{1,0:T(8,128)(2,1)S(1)} %collective-permute-done.7), channel_id=1, source_target_pairs={{0,30},{2,0},{4,2},{6,4},{8,6},{10,8},{12,10},{14,12},{16,14},{18,... | collective-permute-start | bytes 3145736 | tf_op jit(solution)/shard_map/ppermute | solution.py:29
  241.8 27.8 %collective-permute-start.10 = (bf16[4096,128]{1,0:T(8,128)(2,1)S(1)}, bf16[4096,128]{1,0:T(8,128)(2,1)S(1)}, u32[]{:S(2)}, u32[]{:S(2)}) collective-permute-start(bf16[4096,128]{1,0:T(8,128)(2,1)S(1)} %collective-permute-done.8), channel_id=1, source_target_pairs={{0,2},{2,4},{4,6},{6,8},{8,10},{10,12},{12,14},{14,16},{16,18},{18... | collective-permute-start | bytes 3145736 | tf_op jit(solution)/shard_map/ppermute | solution.py:24
  260.6 36.1 %collective-permute-start.11 = (bf16[4096,128]{1,0:T(8,128)(2,1)S(1)}, bf16[4096,128]{1,0:T(8,128)(2,1)S(1)}, u32[]{:S(2)}, u32[]{:S(2)}) collective-permute-start(bf16[4096,128]{1,0:T(8,128)(2,1)S(1)} %collective-permute-done.9), channel_id=1, source_target_pairs={{0,30},{2,0},{4,2},{6,4},{8,6},{10,8},{12,10},{14,12},{16,14},{18,... | collective-permute-start | bytes 3145736 | tf_op jit(solution)/shard_map/ppermute | solution.py:29
  269.6 39.5 %collective-permute-start.12 = (bf16[4096,128]{1,0:T(8,128)(2,1)S(1)}, bf16[4096,128]{1,0:T(8,128)(2,1)S(1)}, u32[]{:S(2)}, u32[]{:S(2)}) collective-permute-start(bf16[4096,128]{1,0:T(8,128)(2,1)S(1)} %collective-permute-done.10), channel_id=1, source_target_pairs={{0,2},{2,4},{4,6},{6,8},{8,10},{10,12},{12,14},{14,16},{16,18},{18... | collective-permute-start | bytes 3145736 | tf_op jit(solution)/shard_map/ppermute | solution.py:24
  270.7 58.6 %copy-start.1 = (bf16[256,2048]{1,0:T(8,128)(2,1)S(1)}, bf16[256,2048]{1,0:T(8,128)(2,1)}, u32[]{:S(2)}) copy-start(bf16[256,2048]{1,0:T(8,128)(2,1)} %param.13) | copy-start | bytes 3145732
  296.7 31.5 %collective-permute-start.13 = (bf16[4096,128]{1,0:T(8,128)(2,1)S(1)}, bf16[4096,128]{1,0:T(8,128)(2,1)S(1)}, u32[]{:S(2)}, u32[]{:S(2)}) collective-permute-start(bf16[4096,128]{1,0:T(8,128)(2,1)S(1)} %collective-permute-done.11), channel_id=1, source_target_pairs={{0,30},{2,0},{4,2},{6,4},{8,6},{10,8},{12,10},{14,12},{16,14},{18,... | collective-permute-start | bytes 3145736 | tf_op jit(solution)/shard_map/ppermute | solution.py:29
  309.1 26.5 %collective-permute-start.14 = (bf16[4096,128]{1,0:T(8,128)(2,1)S(1)}, bf16[4096,128]{1,0:T(8,128)(2,1)}, u32[]{:S(2)}, u32[]{:S(2)}) collective-permute-start(bf16[4096,128]{1,0:T(8,128)(2,1)S(1)} %collective-permute-done.12), channel_id=1, source_target_pairs={{0,2},{2,4},{4,6},{6,8},{8,10},{10,12},{12,14},{14,16},{16,18},{18... | collective-permute-start | bytes 3145736 | tf_op jit(solution)/shard_map/ppermute | solution.py:24
  356.0 3.8 copy-start.9
  374.1 4.1 copy-start.34
  375.8 12.1 copy-start.17
  375.8 5.0 copy-start.15
  387.9 5.1 copy-start.20
  387.9 5.1 copy-start.23
  388.0 5.1 copy-start.25
  388.0 5.1 copy-start.26
  388.0 5.1 copy-start.28
  393.1 19.8 %copy-start.36 = (f32[256,2048]{1,0:T(8,128)S(1)}, f32[256,2048]{1,0:T(8,128)}, u32[]{:S(2)}) copy-start(f32[256,2048]{1,0:T(8,128)} %fusion.90) | copy-start | bytes 6291460
  522.3 12.1 copy-start.2
  534.4 180.2 %reduce-scatter.27.cloned.1.call-start = ((), (), s32[]{:S(2)}) async-start(), calls=%async_computation.17 | async-start | bytes 139264
  538.6 85.9 %copy-start.14 = (bf16[4,256,256]{2,1,0:T(8,128)(2,1)S(1)}, bf16[4,256,256]{2,1,0:T(8,128)(2,1)}, u32[]{:S(2)}) copy-start(bf16[4,256,256]{2,1,0:T(8,128)(2,1)} %copy-done.13) | copy-start | bytes 1572868
  539.6 242.2 %reduce-scatter.25.cloned.1.call-start = ((), (), s32[]{:S(2)}) async-start(), calls=%async_computation.16 | async-start | bytes 1114112
  623.1 175.7 %reduce-scatter.23.cloned.1.call-start = ((), (), s32[]{:S(2)}) async-start(), calls=%async_computation.15 | async-start | bytes 1114112
  624.5 281.5 %reduce-scatter.17.cloned.1.call-start = ((), (), s32[]{:S(2)}) async-start(), calls=%async_computation.12 | async-start | bytes 8912896 | tf_op jit(solution)/shard_map/reduce_scatter | solution.py:267
  629.2 524.4 %reduce-scatter.15.cloned.1.call-start = ((), (), s32[]{:S(2)}) async-start(), calls=%async_computation.11 | async-start | bytes 26738688 | tf_op jit(solution)/shard_map/reduce_scatter | solution.py:265
  643.3 844.8 %reduce-scatter.19.cloned.1.call-start = ((), (), s32[]{:S(2)}) async-start(), calls=%async_computation.13 | async-start | bytes 35651584 | tf_op jit(solution)/shard_map/reduce_scatter | solution.py:269
  658.3 1163.9 %reduce-scatter.21.cloned.1.call-start = ((), (), s32[]{:S(2)}) async-start(), calls=%async_computation.14 | async-start | bytes 35651584 | tf_op jit(solution)/shard_map/reduce_scatter | solution.py:271
  673.1 22.0 %copy-start.33 = (bf16[128]{0:T(256)(128)(2,1)S(1)}, bf16[128]{0:T(256)(128)(2,1)}, u32[]{:S(2)}) copy-start(bf16[128]{0:T(256)(128)(2,1)} %param.23) | copy-start | bytes 772
  673.1 39.5 %copy-start.35 = (u32[32]{0:T(128)S(1)}, u32[32]{0:T(128)}, u32[]{:S(2)}) copy-start(u32[32]{0:T(128)} %constant.200) | copy-start | bytes 388
  673.1 42.9 %copy-start.10 = (bf16[256,2048]{1,0:T(8,128)(2,1)S(1)}, bf16[256,2048]{1,0:T(8,128)(2,1)}, u32[]{:S(2)}) copy-start(bf16[256,2048]{1,0:T(8,128)(2,1)} %get-tuple-element.64) | copy-start | bytes 3145732
  (16 other events, 23.7 us)
Sparse Core Ops, SparseCore 0:
  10.2 64.9 all-gather.8
  77.3 120.4 all-gather.6
  200.0 175.0 all-gather.10
  377.0 134.2 all-gather.12
  534.5 84.0 all-reduce.5
  622.4 55.5 reduce-scatter.26
  681.7 56.6 reduce-scatter.24
  742.0 56.7 reduce-scatter.22
  803.4 102.5 reduce-scatter.16
  910.6 242.9 reduce-scatter.14
  1158.4 329.6 reduce-scatter.18
  1492.7 329.4 reduce-scatter.20
